TPU v7x, 32 devices: a whole 2x2x4 slice. The times are simulated.
32 devices in a mesh: tm: 8 (over z, x), rows: 4 (over y, core).
Axes of the slice: x: 2, y: 2, z: 4, core: 2. Of those that a mesh axis runs over, the one named last changes fastest.
Arguments:
- frames: bfloat16 [8, 32, 64, 128], P('tm', 'rows'), may hold values from -6 to 6
- decays: float32 [8, 256], P('tm'), may hold values from 0.4 to 1
- in_weight: bfloat16 [3, 3, 128, 256], replicated, may hold values from -0.046875 to 0.046875
- out_weight: bfloat16 [3, 3, 256, 128], replicated, may hold values from -0.125 to 0.125
- skip_gain: float32 [128], replicated, may hold values from 0.25 to 1.75
- cotangent: bfloat16 [8, 32, 64, 128], P('tm', 'rows'), may hold values from -6 to 6
Outputs:
- output_frames: bfloat16 [8, 32, 64, 128], P('tm', 'rows')
- input_grad: bfloat16 [8, 32, 64, 128], P('tm', 'rows')
- in_weight_grad: float32 [3, 3, 128, 256], replicated
- out_weight_grad: float32 [3, 3, 256, 128], replicated
- gain_grad: float32 [128], replicated
- decay_grad: float32 [8, 256], P('tm')
All inputs are finite; a program needn't handle non-finite values.
Results may differ from a plain program's by a relative error of at most 0.008.
Values may be sent and summed in bfloat16 or wider, within the bound.
A program may use at most 192 MiB of HBM per device.

v0:
```python
import math
import jax
import jax.numpy as jnp
from jax import lax
from jax.sharding import PartitionSpec as P


def padded_2(block, sides, width):
    for axis, dim in sides:
        count = lax.axis_size(axis)
        forward = [(i, i + 1) for i in range(count - 1)]
        backward = [(target, source) for source, target in forward]
        low = lax.ppermute(
            lax.slice_in_dim(block, block.shape[dim] - width, None, axis=dim), axis, forward
        )
        high = lax.ppermute(lax.slice_in_dim(block, 0, width, axis=dim), axis, backward)
        block = jnp.concatenate([low, block, high], axis=dim)
    return block


def entering(array, axis, join, neutral, backward):
    count = lax.axis_size(axis)
    place = lax.axis_index(axis)
    ahead = count - 1 - place if backward else place
    gathered = jax.tree.map(
        lambda a, kind: lax.all_gather(a.astype(kind), axis), array, (jnp.bfloat16, jnp.bfloat16)
    )
    state = jax.tree.map(lambda a, e: jnp.zeros_like(a) + jnp.asarray(e, a.dtype), array, neutral)

    def one(turn, state):
        source = count - 1 - turn if backward else turn
        return join(
            state,
            jax.tree.map(
                lambda a, own: lax.dynamic_index_in_dim(a, source, 0, False).astype(own.dtype),
                gathered,
                array,
            ),
        )

    return lax.fori_loop(0, ahead, one, state)


def pad_columns(padded_rows):
    return jnp.pad(padded_rows, ((0, 0), (0, 0), (1, 1), (0, 0)))


def conv_taps(padded, weights):
    frame_count = padded.shape[0]
    height = padded.shape[1] - 2
    across = padded.shape[2] - 2
    channels = padded.shape[3]
    result = jnp.zeros((frame_count * height * across, weights.shape[3]), jnp.float32)
    for row_tap in range(3):
        for col_tap in range(3):
            window = padded[:, row_tap : row_tap + height, col_tap : col_tap + across, :].reshape(
                -1, channels
            )
            result = result + jnp.dot(
                window, weights[row_tap, col_tap], preferred_element_type=jnp.float32
            )
    return result.reshape(frame_count, height, across, weights.shape[3])


def tap_grads(padded, grad_field):
    height = grad_field.shape[1]
    across = grad_field.shape[2]
    channels = padded.shape[3]
    flat_grad = grad_field.reshape(-1, grad_field.shape[3])
    outer_list = []
    for row_tap in range(3):
        inner_list = []
        for col_tap in range(3):
            window = padded[:, row_tap : row_tap + height, col_tap : col_tap + across, :].reshape(
                -1, channels
            )
            inner_list.append(
                lax.dot_general(
                    window, flat_grad, (((0,), (0,)), ((), ())), preferred_element_type=jnp.float32
                )
            )
        outer_list.append(jnp.stack(inner_list))
    return jnp.stack(outer_list)


def flipped(weights):
    return jnp.transpose(weights[::-1, ::-1], (0, 1, 3, 2))


def combine(earlier, later):
    return (earlier[0] * later[0], later[0][None, None, :] * earlier[1] + later[1])


def on_device(frames, decays, in_weight, out_weight, skip_gain, cotangent):
    frame_count, band_rows, across, channels = frames.shape
    states_width = in_weight.shape[3]
    total_frames = frame_count * lax.axis_size("tm")
    total_rows = band_rows * lax.axis_size("rows")
    cell_norm = 1.0 / math.sqrt(total_frames * total_rows * across)
    frame_norm = 1.0 / math.sqrt(total_rows * across)
    in_pad = pad_columns(padded_2(frames, (("rows", 1),), 1))
    drive_terms = conv_taps(in_pad, in_weight)

    def forward_step(state, inputs):
        decay_now, drive_now = inputs
        state = decay_now[None, None, :] * state + drive_now
        return (state, state)

    zero_state = jnp.zeros((band_rows, across, states_width), jnp.float32)
    _, local_states = lax.scan(forward_step, zero_state, (decays, drive_terms))
    decay_prefix = jnp.cumprod(decays, axis=0)
    identity = (jnp.ones((states_width,), jnp.float32), zero_state)
    carried = entering((decay_prefix[-1], local_states[-1]), "tm", combine, identity, False)[1]
    states = local_states + decay_prefix[:, None, None, :] * carried[None]
    rounded = states.astype(jnp.bfloat16)
    state_pad = pad_columns(padded_2(rounded, (("rows", 1),), 1))
    output_frames = (
        conv_taps(state_pad, out_weight) + skip_gain * frames.astype(jnp.float32)
    ).astype(jnp.bfloat16)
    cot_pad = pad_columns(padded_2(cotangent, (("rows", 1),), 1))
    from_output = conv_taps(cot_pad, flipped(out_weight))
    next_decay = jnp.concatenate([decays[1:], jnp.zeros((1, states_width), jnp.float32)], axis=0)

    def backward_step(adjoint_now, inputs):
        decay_next, from_now = inputs
        adjoint_now = from_now + decay_next[None, None, :] * adjoint_now
        return (adjoint_now, adjoint_now)

    _, local_adjoint = lax.scan(backward_step, zero_state, (next_decay, from_output), reverse=True)
    later_decay = jnp.concatenate([decays[1:], jnp.ones((1, states_width), jnp.float32)], axis=0)
    decay_suffix = jnp.cumprod(later_decay[::-1], axis=0)[::-1]
    leading = decays[0][None, None, :] * local_adjoint[0]
    incoming = entering((decay_prefix[-1], leading), "tm", combine, identity, True)[1]
    adjoint = local_adjoint + decay_suffix[:, None, None, :] * incoming[None]
    previous = jnp.concatenate([carried[None], states[:-1]], axis=0)
    decay_terms = jnp.sum(adjoint * previous, axis=(1, 2)) * frame_norm
    adjoint_low = adjoint.astype(jnp.bfloat16)
    in_grad_terms = tap_grads(in_pad, adjoint_low) * cell_norm
    out_grad_terms = tap_grads(state_pad, cotangent) * cell_norm
    gain_terms = (
        jnp.sum(cotangent.astype(jnp.float32) * frames.astype(jnp.float32), axis=(0, 1, 2))
        * cell_norm
    )
    adjoint_pad = pad_columns(padded_2(adjoint_low, (("rows", 1),), 1))
    input_grad = (
        conv_taps(adjoint_pad, flipped(in_weight)) + skip_gain * cotangent.astype(jnp.float32)
    ).astype(jnp.bfloat16)
    in_weight_grad, out_weight_grad, gain_grad = lax.psum(
        (in_grad_terms, out_grad_terms, gain_terms), ("tm", "rows")
    )
    decay_grad = lax.psum(decay_terms, "rows")
    return (output_frames, input_grad, in_weight_grad, out_weight_grad, gain_grad, decay_grad)


def solution(mesh):
    in_specs = (
        P("tm", "rows", None, None),
        P("tm", None),
        P(),
        P(),
        P(),
        P("tm", "rows", None, None),
    )
    out_specs = (
        P("tm", "rows", None, None),
        P("tm", "rows", None, None),
        P(),
        P(),
        P(),
        P("tm", None),
    )
    return jax.shard_map(
        on_device, mesh=mesh, in_specs=in_specs, out_specs=out_specs, check_vma=False
    )
```

profile of v0, /device:TPU:0, one launch (start us, length us, event | category | flops | bytes accessed | tf_op | source)
XLA Modules:
  0.0 304.3 jit_solution(4210442601135215782)
XLA Ops:
  8.0 1.3 collective-permute-start.1
  9.3 3.0 collective-permute-start
  17.4 1.3 collective-permute-start.5
  18.8 5.1 %collective-permute-start.4 = (bf16[1,1,64,128]{3,2,1,0:T(8,128)(2,1)S(1)}, bf16[1,1,64,128]{3,2,1,0:T(8,128)(2,1)S(1)}, u32[]{:S(2)}, u32[]{:S(2)}) collective-permute-start(bf16[1,1,64,128]{3,2,1,0:T(8,128)(2,1)S(1)} %get-tuple-element.225), channel_id=1, source_target_pairs={{0,1},{1,2},{2,3},{4,5},{5,6},{6,7},{8,9},{9,10},{10,11},{12,13},{... | collective-permute-start | bytes 49160 | tf_op jit(solution)/shard_map/ppermute | solution.py:13
  28.4 20.8 %all-gather = bf16[8,1,256]{2,1,0:T(2,128)(2,1)S(1)} all-gather(bf16[1,1,256]{2,1,0:T(2,128)(2,1)S(1)} %convert_bitcast_fusion), channel_id=1, replica_groups=mesh['tm'=8,'rows'=4] {'tm'}, dimensions={0}, use_global_device_ids=true | all-gather | bytes 4608 | tf_op jit(solution)/shard_map/all_gather | solution.py:26
  50.1 21.5 %all-gather.4.cloned.1.call-done = bf16[8,8,64,256]{3,2,1,0:T(8,128)(2,1)} async-done(((bf16[1,8,64,256]{3,2,1,0:T(8,128)(2,1)}), bf16[8,8,64,256]{3,2,1,0:T(8,128)(2,1)}) %all-gather.4.cloned.1.call-update) | async-done | bytes 2097168 | tf_op jit(solution)/shard_map/all_gather | solution.py:26
  71.6 49.9 %all-gather.6.cloned.1.call-done = bf16[8,8,64,256]{3,2,1,0:T(8,128)(2,1)} async-done(((bf16[1,8,64,256]{3,2,1,0:T(8,128)(2,1)}), bf16[8,8,64,256]{3,2,1,0:T(8,128)(2,1)}) %all-gather.6.cloned.1.call-update) | async-done | bytes 2097168 | tf_op jit(solution)/shard_map/all_gather | solution.py:26
  121.5 8.5 %while.17 = (s32[]{:T(128)}, f32[8,64,256]{2,1,0:T(8,128)S(1)}, s32[]{:T(128)}, bf16[8,256]{1,0:T(8,128)(2,1)S(1)}, bf16[8,8,64,256]{3,2,1,0:T(8,128)(2,1)}, /*index=5*/s32[]{:T(128)}, s32[]{:T(128)}, s32[]{:T(128)}, s32[]{:T(128)}) while((s32[]{:T(128)}, f32[8,64,256]{2,1,0:T(8,128)S(1)}, s32[]{:T(128)}, bf16[8,256]{1,0:T(8,128)(2,1)S(1)}, ...), condition=%wide.region_4.5_spmd, body=%wide.region_3.4_spmd.sunk | while | flops 393478 | bytes 1313435 | solution.py:41
  121.6 1.2 convert_add_fusion.5
  122.8 1.2 convert_add_fusion.5
  124.0 1.2 convert_add_fusion.5
  125.2 1.2 convert_add_fusion.5
  126.4 1.2 convert_add_fusion.5
  127.6 1.2 convert_add_fusion.5
  128.9 1.2 convert_add_fusion.5
  132.4 1.3 collective-permute-start.7
  133.7 3.0 collective-permute-start.6
  137.0 1.3 collective-permute-start.3
  138.3 3.6 %collective-permute-start.2 = (bf16[1,1,64,256]{3,2,1,0:T(8,128)(2,1)S(1)}, bf16[1,1,64,256]{3,2,1,0:T(8,128)(2,1)S(1)}, u32[]{:S(2)}, u32[]{:S(2)}) collective-permute-start(bf16[1,1,64,256]{3,2,1,0:T(8,128)(2,1)S(1)} %get-tuple-element.206), channel_id=1, source_target_pairs={{0,1},{1,2},{2,3},{4,5},{5,6},{6,7},{8,9},{9,10},{10,11},{12,13},{... | collective-permute-start | bytes 98312 | tf_op jit(solution)/shard_map/ppermute | solution.py:13
  142.0 1.1 maximum_multiply_fusion
  143.2 7.9 %psum.31 = f32[1,256]{1,0:T(1,128)} all-reduce(f32[1,256]{1,0:T(1,128)S(1)} %bitcast.421), channel_id=1, replica_groups=mesh['tm'=8,'rows'=4] {'rows'}, use_global_device_ids=true, to_apply=%region_10.11 | all-reduce | flops 256 | bytes 2048 | tf_op jit(solution)/shard_map/psum | solution.py:151
  163.2 37.1 %psum.30 = f32[128]{0:T(128)} all-reduce(f32[128]{0:T(128)S(1)} %broadcast_multiply_fusion.2), channel_id=1, replica_groups=mesh['tm'=8,'rows'=4] {'tm','rows'}, use_global_device_ids=true, to_apply=%region_8.9 | all-reduce | flops 128 | bytes 1024 | tf_op jit(solution)/shard_map/psum | solution.py:148
  200.3 94.0 %all-reduce.7.cloned.1.call-done = (f32[3,3,128,256]{3,2,1,0:T(8,128)}, f32[3,3,256,128]{3,2,1,0:T(8,128)}) async-done(((f32[3,3,128,256]{3,2,1,0:T(8,128)}, f32[3,3,256,128]{3,2,1,0:T(8,128)}), (f32[3,3,128,256]{3,2,1,0:T(8,128)}, f32[3,3,256,128]{3,2,1,0:T(8,128)})) %all-reduce.7.cloned.1.call-update) | async-done | bytes 2359312 | tf_op jit(solution)/shard_map/psum | solution.py:148
  294.3 2.5 copy.34
  (134 shorter events, 26.7 us)
Async XLA Ops:
  7.2 7.1 %copy-start.2 = (bf16[3,3,128,256]{3,2,1,0:T(8,128)(2,1)S(1)}, bf16[3,3,128,256]{3,2,1,0:T(8,128)(2,1)}, u32[]{:S(2)}) copy-start(bf16[3,3,128,256]{3,2,1,0:T(8,128)(2,1)} %param.12) | copy-start | bytes 1769476
  7.2 64.4 %all-gather.4.cloned.1.call-start = ((), (), s32[]{:S(2)}) async-start(), calls=%async_computation | async-start | bytes 2359296 | tf_op jit(solution)/shard_map/all_gather | solution.py:26
  8.0 5.0 %collective-permute-start.1 = (bf16[1,1,64,128]{3,2,1,0:T(8,128)(2,1)S(1)}, bf16[1,1,64,128]{3,2,1,0:T(8,128)(2,1)S(1)}, u32[]{:S(2)}, u32[]{:S(2)}) collective-permute-start(bf16[1,1,64,128]{3,2,1,0:T(8,128)(2,1)S(1)} %get-tuple-element.230), channel_id=1, source_target_pairs={{1,0},{2,1},{3,2},{5,4},{6,5},{7,6},{9,8},{10,9},{11,10},{13,12},{... | collective-permute-start | bytes 49160 | tf_op jit(solution)/shard_map/ppermute | solution.py:16
  9.3 3.9 %collective-permute-start = (bf16[1,1,64,128]{3,2,1,0:T(8,128)(2,1)S(1)}, bf16[1,1,64,128]{3,2,1,0:T(8,128)(2,1)S(1)}, u32[]{:S(2)}, u32[]{:S(2)}) collective-permute-start(bf16[1,1,64,128]{3,2,1,0:T(8,128)(2,1)S(1)} %get-tuple-element.229), channel_id=1, source_target_pairs={{0,1},{1,2},{2,3},{4,5},{5,6},{6,7},{8,9},{9,10},{10,11},{12,13},{... | collective-permute-start | bytes 49160 | tf_op jit(solution)/shard_map/ppermute | solution.py:13
  14.1 0.9 copy-start.1
  16.4 1.1 copy-start
  16.4 7.5 %copy-start.3 = (bf16[3,3,256,128]{3,2,1,0:T(8,128)(2,1)S(1)}, bf16[3,3,256,128]{3,2,1,0:T(8,128)(2,1)}, u32[]{:S(2)}) copy-start(bf16[3,3,256,128]{3,2,1,0:T(8,128)(2,1)} %param.13) | copy-start | bytes 1769476
  17.4 104.1 %all-gather.6.cloned.1.call-start = ((), (), s32[]{:S(2)}) async-start(), calls=%async_computation.1 | async-start | bytes 2359296 | tf_op jit(solution)/shard_map/all_gather | solution.py:26
  17.4 6.5 %collective-permute-start.5 = (bf16[1,1,64,128]{3,2,1,0:T(8,128)(2,1)S(1)}, bf16[1,1,64,128]{3,2,1,0:T(8,128)(2,1)S(1)}, u32[]{:S(2)}, u32[]{:S(2)}) collective-permute-start(bf16[1,1,64,128]{3,2,1,0:T(8,128)(2,1)S(1)} %get-tuple-element.226), channel_id=1, source_target_pairs={{1,0},{2,1},{3,2},{5,4},{6,5},{7,6},{9,8},{10,9},{11,10},{13,12},{... | collective-permute-start | bytes 49160 | tf_op jit(solution)/shard_map/ppermute | solution.py:16
  18.8 6.0 %collective-permute-start.4 = (bf16[1,1,64,128]{3,2,1,0:T(8,128)(2,1)S(1)}, bf16[1,1,64,128]{3,2,1,0:T(8,128)(2,1)S(1)}, u32[]{:S(2)}, u32[]{:S(2)}) collective-permute-start(bf16[1,1,64,128]{3,2,1,0:T(8,128)(2,1)S(1)} %get-tuple-element.225), channel_id=1, source_target_pairs={{0,1},{1,2},{2,3},{4,5},{5,6},{6,7},{8,9},{9,10},{10,11},{12,13},{... | collective-permute-start | bytes 49160 | tf_op jit(solution)/shard_map/ppermute | solution.py:13
  26.8 0.7 copy-start.9
  28.3 266.0 %all-reduce.7.cloned.1.call-start = ((), (), s32[]{:S(2)}) async-start(), calls=%async_computation.2 | async-start | bytes 4718592 | tf_op jit(solution)/shard_map/psum | solution.py:148
  132.4 20.7 %collective-permute-start.7 = (bf16[1,1,64,256]{3,2,1,0:T(8,128)(2,1)S(1)}, bf16[1,1,64,256]{3,2,1,0:T(8,128)(2,1)S(1)}, u32[]{:S(2)}, u32[]{:S(2)}) collective-permute-start(bf16[1,1,64,256]{3,2,1,0:T(8,128)(2,1)S(1)} %get-tuple-element.203), channel_id=1, source_target_pairs={{1,0},{2,1},{3,2},{5,4},{6,5},{7,6},{9,8},{10,9},{11,10},{13,12},{... | collective-permute-start | bytes 98312 | tf_op jit(solution)/shard_map/ppermute | solution.py:16
  133.7 19.4 %collective-permute-start.6 = (bf16[1,1,64,256]{3,2,1,0:T(8,128)(2,1)S(1)}, bf16[1,1,64,256]{3,2,1,0:T(8,128)(2,1)S(1)}, u32[]{:S(2)}, u32[]{:S(2)}) collective-permute-start(bf16[1,1,64,256]{3,2,1,0:T(8,128)(2,1)S(1)} %get-tuple-element.202), channel_id=1, source_target_pairs={{0,1},{1,2},{2,3},{4,5},{5,6},{6,7},{8,9},{9,10},{10,11},{12,13},{... | collective-permute-start | bytes 98312 | tf_op jit(solution)/shard_map/ppermute | solution.py:13
  137.0 14.1 %collective-permute-start.3 = (bf16[1,1,64,256]{3,2,1,0:T(8,128)(2,1)S(1)}, bf16[1,1,64,256]{3,2,1,0:T(8,128)(2,1)S(1)}, u32[]{:S(2)}, u32[]{:S(2)}) collective-permute-start(bf16[1,1,64,256]{3,2,1,0:T(8,128)(2,1)S(1)} %get-tuple-element.207), channel_id=1, source_target_pairs={{1,0},{2,1},{3,2},{5,4},{6,5},{7,6},{9,8},{10,9},{11,10},{13,12},{... | collective-permute-start | bytes 98312 | tf_op jit(solution)/shard_map/ppermute | solution.py:16
  138.3 12.8 %collective-permute-start.2 = (bf16[1,1,64,256]{3,2,1,0:T(8,128)(2,1)S(1)}, bf16[1,1,64,256]{3,2,1,0:T(8,128)(2,1)S(1)}, u32[]{:S(2)}, u32[]{:S(2)}) collective-permute-start(bf16[1,1,64,256]{3,2,1,0:T(8,128)(2,1)S(1)} %get-tuple-element.206), channel_id=1, source_target_pairs={{0,1},{1,2},{2,3},{4,5},{5,6},{6,7},{8,9},{9,10},{10,11},{12,13},{... | collective-permute-start | bytes 98312 | tf_op jit(solution)/shard_map/ppermute | solution.py:13
  153.1 1.1 copy-start.5
  153.4 1.3 copy-start.4
  161.0 0.9 copy-start.7
  161.0 1.2 copy-start.8
  161.2 1.2 copy-start.10
  294.3 2.5 copy-start.6
Sparse Core Ops, SparseCore 0:
  17.5 53.9 all-gather.3
  73.7 47.7 all-gather.5
  161.1 133.1 all-reduce.6
where the time goes:
time: 305 us; the launch traced here: 304 us
  waiting for transfers between devices  166 us (54%)
  blocking collectives  65.8 us (22%)
  starting transfers between devices  20.1 us (7%)
  other arithmetic  15.3 us (5%)
  between operations  14.4 us (5%)
  matrix products  13.9 us (5%)
  local copies, waits for them, and re-layouts  8.25 us (3%)
    psum x1, waiting for transfers between devices, on_device(): lax.psum((in_grad_terms, out_grad_terms, gain_terms), ('tm', 'rows'))  94 us
    all_gather x2, waiting for transfers between devices, entering(): lax.all_gather(a.astype(kind), axis)  71.4 us
    psum x1, blocking collectives, on_device(): lax.psum((in_grad_terms, out_grad_terms, gain_terms), ('tm', 'rows'))  37.1 us
    all_gather x1, blocking collectives, entering(): lax.all_gather(a.astype(kind), axis)  20.8 us
    ppermute x4, starting transfers between devices, padded_2(): lax.ppermute(lax.slice_in_dim(block, block.shape[dim] - width, None, axis...  14.8 us
    dot_general x36, matrix products, conv_taps(): jnp.dot(window, weights[row_tap, col_tap], preferred_element_type=jnp.flo...  9.44 us
    add x7, other arithmetic, combine(): later[0][None, None, :] * earlier[1] + later[1]  8.23 us
    psum x1, blocking collectives, on_device(): decay_grad = lax.psum(decay_terms, 'rows')  7.91 us
  transfers between devices with their start and end apart: 11, of which 5 were waited for; matrix products, arithmetic and copies ran while one was open for 3% of the time, Pallas kernels for 0%

commit v1 on v0

--- a/solution.py
+++ b/solution.py
@@ -1,8 +1,17 @@
+import functools
 import math
 import jax
 import jax.numpy as jnp
 from jax import lax
 from jax.sharding import PartitionSpec as P
+
+
+def _run_axis_part(s0, axis_key, dev_axis):
+    then = lax.psum(s0, axis_name=axis_key)
+    return lax.psum(then, axis_name=dev_axis)
+
+
+raise_sheet = functools.partial(_run_axis_part, axis_key="rows", dev_axis="tm")
 
 
 def padded_2(block, sides, width):
@@ -145,8 +154,8 @@
     input_grad = (
         conv_taps(adjoint_pad, flipped(in_weight)) + skip_gain * cotangent.astype(jnp.float32)
     ).astype(jnp.bfloat16)
-    in_weight_grad, out_weight_grad, gain_grad = lax.psum(
-        (in_grad_terms, out_grad_terms, gain_terms), ("tm", "rows")
+    in_weight_grad, out_weight_grad, gain_grad = raise_sheet(
+        (in_grad_terms, out_grad_terms, gain_terms)
     )
     decay_grad = lax.psum(decay_terms, "rows")
     return (output_frames, input_grad, in_weight_grad, out_weight_grad, gain_grad, decay_grad)

time: 305 us -> 331 us (1.085)
  waiting for transfers between devices: 166 us -> 207 us
  blocking collectives: 65.8 us -> 50.6 us
  local copies, waits for them, and re-layouts: 8.25 us -> 11.6 us
    psum x1 -> x2, waiting for transfers between devices: 94 us -> 141 us  [the longest x1 78.8 us: _run_axis_part(): return lax.psum(then, axis_name=dev_axis)]
    psum x2, blocking collectives: 45 us -> 29.8 us  [the longest x1 23.5 us: _run_axis_part(): return lax.psum(then, axis_name=dev_axis)]
    all_gather x2, waiting for transfers between devices: 71.4 us -> 61.6 us  [entering(): lax.all_gather(a.astype(kind), axis)]
    ppermute x4, waiting for transfers between devices: 0.01 us -> 4.56 us  [padded_2(): lax.ppermute(lax.slice_in_dim(block, 0, width, axis=dim), axis, backward)]
  transfers between devices with their start and end apart: 11 -> 12, of which waited for: 5 -> 6; matrix products, arithmetic and copies ran while one was open for 3% -> 7% of each run, Pallas kernels for 0% -> 0%
where the time goes in v1:
time: 331 us
  waiting for transfers between devices  207 us (63%)
  blocking collectives  50.6 us (15%)
  starting transfers between devices  18.2 us (5%)
  between operations  14.5 us (4%)
  other arithmetic  14.4 us (4%)
  matrix products  13.8 us (4%)
  local copies, waits for them, and re-layouts  11.6 us (4%)
    psum x1, waiting for transfers between devices, _run_axis_part(): return lax.psum(then, axis_name=dev_axis)  78.8 us
    psum x1, waiting for transfers between devices, _run_axis_part(): then = lax.psum(s0, axis_name=axis_key)  62.3 us
    all_gather x2, waiting for transfers between devices, entering(): lax.all_gather(a.astype(kind), axis)  61.6 us
    psum x1, blocking collectives, _run_axis_part(): return lax.psum(then, axis_name=dev_axis)  23.5 us
    all_gather x1, blocking collectives, entering(): lax.all_gather(a.astype(kind), axis)  20.8 us
    ppermute x4, starting transfers between devices, padded_2(): lax.ppermute(lax.slice_in_dim(block, block.shape[dim] - width, None, axis...  12.9 us
    dot_general x36, matrix products, conv_taps(): jnp.dot(window, weights[row_tap, col_tap], preferred_element_type=jnp.flo...  9.39 us
    add x7, other arithmetic, combine(): later[0][None, None, :] * earlier[1] + later[1]  8.23 us
  transfers between devices with their start and end apart: 12, of which 6 were waited for; matrix products, arithmetic and copies ran while one was open for 7% of the time, Pallas kernels for 0%

profile of v1, /device:TPU:0, one launch (start us, length us, event | category | flops | bytes accessed | tf_op | source)
XLA Modules:
  0.0 330.7 jit_solution(649604095282102272)
XLA Ops:
  8.0 2.3 collective-permute-start.4
  10.3 1.3 collective-permute-start.5
  12.8 2.8 collective-permute-done.5
  19.2 4.5 %collective-permute-start = (bf16[1,1,64,128]{3,2,1,0:T(8,128)(2,1)S(1)}, bf16[1,1,64,128]{3,2,1,0:T(8,128)(2,1)S(1)}, u32[]{:S(2)}, u32[]{:S(2)}) collective-permute-start(bf16[1,1,64,128]{3,2,1,0:T(8,128)(2,1)S(1)} %get-tuple-element.233), channel_id=1, source_target_pairs={{0,1},{1,2},{2,3},{4,5},{5,6},{6,7},{8,9},{9,10},{10,11},{12,13},{... | collective-permute-start | bytes 49160 | tf_op jit(solution)/shard_map/ppermute | solution.py:22
  23.7 1.3 collective-permute-start.1
  25.0 1.8 collective-permute-done.1
  29.8 20.8 %all-gather = bf16[8,1,256]{2,1,0:T(2,128)(2,1)S(1)} all-gather(bf16[1,1,256]{2,1,0:T(2,128)(2,1)S(1)} %convert_bitcast_fusion), channel_id=1, replica_groups=mesh['tm'=8,'rows'=4] {'tm'}, dimensions={0}, use_global_device_ids=true | all-gather | bytes 4608 | tf_op jit(solution)/shard_map/all_gather | solution.py:35
  51.5 19.6 %all-gather.6.cloned.1.call-done = bf16[8,8,64,256]{3,2,1,0:T(8,128)(2,1)} async-done(((bf16[1,8,64,256]{3,2,1,0:T(8,128)(2,1)}), bf16[8,8,64,256]{3,2,1,0:T(8,128)(2,1)}) %all-gather.6.cloned.1.call-update) | async-done | bytes 2097168 | tf_op jit(solution)/shard_map/all_gather | solution.py:35
  71.2 8.5 %while.17 = (s32[]{:T(128)}, f32[8,64,256]{2,1,0:T(8,128)S(1)}, s32[]{:T(128)}, bf16[8,256]{1,0:T(8,128)(2,1)S(1)}, bf16[8,8,64,256]{3,2,1,0:T(8,128)(2,1)}, /*index=5*/s32[]{:T(128)}, s32[]{:T(128)}, s32[]{:T(128)}, s32[]{:T(128)}) while((s32[]{:T(128)}, f32[8,64,256]{2,1,0:T(8,128)S(1)}, s32[]{:T(128)}, bf16[8,256]{1,0:T(8,128)(2,1)S(1)}, ...), condition=%wide.region_4.5_spmd, body=%wide.region_3.4_spmd.sunk | while | flops 393478 | bytes 1313427 | solution.py:50
  71.2 1.2 convert_add_fusion.5
  74.9 1.2 convert_add_fusion.5
  76.1 1.2 convert_add_fusion.5
  78.5 1.2 convert_add_fusion.5
  79.7 41.9 %all-gather.4.cloned.1.call-done = bf16[8,8,64,256]{3,2,1,0:T(8,128)(2,1)} async-done(((bf16[1,8,64,256]{3,2,1,0:T(8,128)(2,1)}), bf16[8,8,64,256]{3,2,1,0:T(8,128)(2,1)}) %all-gather.4.cloned.1.call-update) | async-done | bytes 2097168 | tf_op jit(solution)/shard_map/all_gather | solution.py:35
  124.3 1.3 collective-permute-start.2
  125.6 1.3 collective-permute-start.3
  126.9 4.7 %collective-permute-start.6 = (bf16[1,1,64,256]{3,2,1,0:T(8,128)(2,1)S(1)}, bf16[1,1,64,256]{3,2,1,0:T(8,128)(2,1)S(1)}, u32[]{:S(2)}, u32[]{:S(2)}) collective-permute-start(bf16[1,1,64,256]{3,2,1,0:T(8,128)(2,1)S(1)} %get-tuple-element.206), channel_id=1, source_target_pairs={{0,1},{1,2},{2,3},{4,5},{5,6},{6,7},{8,9},{9,10},{10,11},{12,13},{... | collective-permute-start | bytes 98312 | tf_op jit(solution)/shard_map/ppermute | solution.py:22
  131.7 1.3 collective-permute-start.7
  137.7 1.3 fusion.95
  145.4 62.3 %all-reduce.12.cloned.1.call-done = (f32[3,3,128,256]{3,2,1,0:T(8,128)}, f32[3,3,256,128]{3,2,1,0:T(8,128)}) async-done(((f32[3,3,128,256]{3,2,1,0:T(8,128)}, f32[3,3,256,128]{3,2,1,0:T(8,128)}), (f32[3,3,128,256]{3,2,1,0:T(8,128)}, f32[3,3,256,128]{3,2,1,0:T(8,128)})) %all-reduce.12.cloned.1.call-update) | async-done | bytes 2359312 | tf_op jit(solution)/shard_map/psum | solution.py:10
  212.1 6.3 %all-reduce.5 = (f32[128]{0:T(128)S(1)}, f32[1,256]{1,0:T(1,128)}) all-reduce(f32[128]{0:T(128)S(1)} %broadcast_multiply_fusion.2, f32[1,256]{1,0:T(1,128)S(1)} %bitcast.421), channel_id=1, replica_groups=mesh['tm'=8,'rows'=4] {'rows'}, use_global_device_ids=true, to_apply=%region_10.11 | all-reduce | flops 384 | bytes 3072 | tf_op jit(solution)/shard_map/psum | solution.py:10
  218.4 23.5 %psum.54 = f32[128]{0:T(128)} all-reduce(f32[128]{0:T(128)S(1)} %get-tuple-element.185), channel_id=1, replica_groups=mesh['tm'=8,'rows'=4] {'tm'}, use_global_device_ids=true, to_apply=%region_11.12 | all-reduce | flops 128 | bytes 1024 | tf_op jit(solution)/shard_map/psum | solution.py:11
  241.9 78.8 %all-reduce.10.cloned.1.call-done = (f32[3,3,128,256]{3,2,1,0:T(8,128)}, f32[3,3,256,128]{3,2,1,0:T(8,128)}) async-done(((f32[3,3,128,256]{3,2,1,0:T(8,128)}, f32[3,3,256,128]{3,2,1,0:T(8,128)}), (f32[3,3,128,256]{3,2,1,0:T(8,128)}, f32[3,3,256,128]{3,2,1,0:T(8,128)})) %all-reduce.10.cloned.1.call-update) | async-done | bytes 2359312 | tf_op jit(solution)/shard_map/psum | solution.py:11
  320.7 2.5 copy.36
  (153 shorter events, 31.6 us)
Async XLA Ops:
  7.2 8.4 %copy-start = (bf16[1,8,64,128]{3,2,1,0:T(8,128)(2,1)S(1)}, bf16[1,8,64,128]{3,2,1,0:T(8,128)(2,1)}, u32[]{:S(2)}) copy-start(bf16[1,8,64,128]{3,2,1,0:T(8,128)(2,1)} %param.15) | copy-start | bytes 393220
  7.2 64.0 %all-gather.6.cloned.1.call-start = ((), (), s32[]{:S(2)}) async-start(), calls=%async_computation.1 | async-start | bytes 2359296 | tf_op jit(solution)/shard_map/all_gather | solution.py:35
  8.0 4.8 %collective-permute-start.4 = (bf16[1,1,64,128]{3,2,1,0:T(8,128)(2,1)S(1)}, bf16[1,1,64,128]{3,2,1,0:T(8,128)(2,1)S(1)}, u32[]{:S(2)}, u32[]{:S(2)}) collective-permute-start(bf16[1,1,64,128]{3,2,1,0:T(8,128)(2,1)S(1)} %get-tuple-element.229), channel_id=1, source_target_pairs={{0,1},{1,2},{2,3},{4,5},{5,6},{6,7},{8,9},{9,10},{10,11},{12,13},{... | collective-permute-start | bytes 49160 | tf_op jit(solution)/shard_map/ppermute | solution.py:22
  10.3 5.2 %collective-permute-start.5 = (bf16[1,1,64,128]{3,2,1,0:T(8,128)(2,1)S(1)}, bf16[1,1,64,128]{3,2,1,0:T(8,128)(2,1)S(1)}, u32[]{:S(2)}, u32[]{:S(2)}) collective-permute-start(bf16[1,1,64,128]{3,2,1,0:T(8,128)(2,1)S(1)} %get-tuple-element.230), channel_id=1, source_target_pairs={{1,0},{2,1},{3,2},{5,4},{6,5},{7,6},{9,8},{10,9},{11,10},{13,12},{... | collective-permute-start | bytes 49160 | tf_op jit(solution)/shard_map/ppermute | solution.py:25
  17.7 1.5 copy-start.1
  19.1 102.5 %all-gather.4.cloned.1.call-start = ((), (), s32[]{:S(2)}) async-start(), calls=%async_computation | async-start | bytes 2359296 | tf_op jit(solution)/shard_map/all_gather | solution.py:35
  19.2 7.8 %copy-start.2 = (bf16[3,3,128,256]{3,2,1,0:T(8,128)(2,1)S(1)}, bf16[3,3,128,256]{3,2,1,0:T(8,128)(2,1)}, u32[]{:S(2)}) copy-start(bf16[3,3,128,256]{3,2,1,0:T(8,128)(2,1)} %param.12) | copy-start | bytes 1769476
  19.2 5.8 %collective-permute-start = (bf16[1,1,64,128]{3,2,1,0:T(8,128)(2,1)S(1)}, bf16[1,1,64,128]{3,2,1,0:T(8,128)(2,1)S(1)}, u32[]{:S(2)}, u32[]{:S(2)}) collective-permute-start(bf16[1,1,64,128]{3,2,1,0:T(8,128)(2,1)S(1)} %get-tuple-element.233), channel_id=1, source_target_pairs={{0,1},{1,2},{2,3},{4,5},{5,6},{6,7},{8,9},{9,10},{10,11},{12,13},{... | collective-permute-start | bytes 49160 | tf_op jit(solution)/shard_map/ppermute | solution.py:22
  23.7 3.1 collective-permute-start.1
  29.8 177.9 %all-reduce.12.cloned.1.call-start = ((), (), s32[]{:S(2)}) async-start(), calls=%async_computation.3 | async-start | bytes 4718592 | tf_op jit(solution)/shard_map/psum | solution.py:10
  124.3 9.9 %collective-permute-start.2 = (bf16[1,1,64,256]{3,2,1,0:T(8,128)(2,1)S(1)}, bf16[1,1,64,256]{3,2,1,0:T(8,128)(2,1)S(1)}, u32[]{:S(2)}, u32[]{:S(2)}) collective-permute-start(bf16[1,1,64,256]{3,2,1,0:T(8,128)(2,1)S(1)} %get-tuple-element.210), channel_id=1, source_target_pairs={{0,1},{1,2},{2,3},{4,5},{5,6},{6,7},{8,9},{9,10},{10,11},{12,13},{... | collective-permute-start | bytes 98312 | tf_op jit(solution)/shard_map/ppermute | solution.py:22
  125.6 8.6 %collective-permute-start.3 = (bf16[1,1,64,256]{3,2,1,0:T(8,128)(2,1)S(1)}, bf16[1,1,64,256]{3,2,1,0:T(8,128)(2,1)S(1)}, u32[]{:S(2)}, u32[]{:S(2)}) collective-permute-start(bf16[1,1,64,256]{3,2,1,0:T(8,128)(2,1)S(1)} %get-tuple-element.211), channel_id=1, source_target_pairs={{1,0},{2,1},{3,2},{5,4},{6,5},{7,6},{9,8},{10,9},{11,10},{13,12},{... | collective-permute-start | bytes 98312 | tf_op jit(solution)/shard_map/ppermute | solution.py:25
  126.9 10.7 %collective-permute-start.6 = (bf16[1,1,64,256]{3,2,1,0:T(8,128)(2,1)S(1)}, bf16[1,1,64,256]{3,2,1,0:T(8,128)(2,1)S(1)}, u32[]{:S(2)}, u32[]{:S(2)}) collective-permute-start(bf16[1,1,64,256]{3,2,1,0:T(8,128)(2,1)S(1)} %get-tuple-element.206), channel_id=1, source_target_pairs={{0,1},{1,2},{2,3},{4,5},{5,6},{6,7},{8,9},{9,10},{10,11},{12,13},{... | collective-permute-start | bytes 98312 | tf_op jit(solution)/shard_map/ppermute | solution.py:22
  131.7 5.9 %collective-permute-start.7 = (bf16[1,1,64,256]{3,2,1,0:T(8,128)(2,1)S(1)}, bf16[1,1,64,256]{3,2,1,0:T(8,128)(2,1)S(1)}, u32[]{:S(2)}, u32[]{:S(2)}) collective-permute-start(bf16[1,1,64,256]{3,2,1,0:T(8,128)(2,1)S(1)} %get-tuple-element.207), channel_id=1, source_target_pairs={{1,0},{2,1},{3,2},{5,4},{6,5},{7,6},{9,8},{10,9},{11,10},{13,12},{... | collective-permute-start | bytes 98312 | tf_op jit(solution)/shard_map/ppermute | solution.py:25
  135.8 1.1 copy-start.3
  142.2 1.2 copy-start.4
  142.2 1.3 copy-start.14
  142.2 1.7 copy-start.12
  142.2 178.5 %all-reduce.10.cloned.1.call-start = ((), (), s32[]{:S(2)}) async-start(), calls=%async_computation.2 | async-start | bytes 4718592 | tf_op jit(solution)/shard_map/psum | solution.py:11
  142.3 1.4 copy-start.16
  143.0 1.2 copy-start.11
  207.7 1.2 copy-start.9
  207.7 1.4 copy-start.8
  320.7 2.5 copy-start.5
  (7 other events, 6.5 us)
Sparse Core Ops, SparseCore 0:
  19.2 51.8 all-gather.5
  73.8 47.7 all-gather.3
  142.3 65.3 all-reduce.11
  211.2 109.4 all-reduce.9
